TPU v7x, 32 devices: a whole 2x2x4 slice. The times are simulated.
32 devices in a mesh: seg: 4 (over z), mem: 8 (over y, x, core).
Axes of the slice: x: 2, y: 2, z: 4, core: 2. Of those that a mesh axis runs over, the one named last changes fastest.
Arguments:
- tokens: bfloat16 [8192, 1024], P(('seg', 'mem')), may hold values from -6 to 6
- padding_mask: int32 [8192], P(('seg', 'mem')), may hold values from 0 to 1, as said below
- memory_keys: bfloat16 [4, 8192, 1024], P('seg', 'mem'), may hold values from -6 to 6
- memory_values: bfloat16 [4, 8192, 1024], P('seg', 'mem'), may hold values from -6 to 6
- memory_length: int32 [4], P('seg'), may hold values from 2048 to 8192, as said below
- chosen_keys: int32 [16, 128], P('seg'), may hold values from 0 to 8191, as said below
- norm_gain: float32 [1024], replicated, may hold values from 0.1 to 1.9
- w_query: bfloat16 [1024, 1024], replicated, may hold values from -0.1875 to 0.1875
- w_key: bfloat16 [1024, 1024], replicated, may hold values from -0.1875 to 0.1875
- w_value: bfloat16 [1024, 1024], replicated, may hold values from -0.1875 to 0.1875
- w_out: bfloat16 [1024, 1024], replicated, may hold values from -1.5 to 1.5
- ffn_gain: float32 [1024], replicated, may hold values from 0.1 to 1.9
- w_gate: bfloat16 [1024, 2816], replicated, may hold values from -0.1875 to 0.1875
- w_up: bfloat16 [1024, 2816], replicated, may hold values from -0.1875 to 0.1875
- w_down: bfloat16 [2816, 1024], replicated, may hold values from -0.109375 to 0.109375
- cotangent: bfloat16 [8192, 1024], P(('seg', 'mem')), may hold values from -6 to 6
Outputs:
- mixed: bfloat16 [8192, 1024], P(('seg', 'mem'))
- input_grad: bfloat16 [8192, 1024], P(('seg', 'mem'))
- norm_gain_grad: float32 [1024], P('mem')
- query_grad: float32 [1024, 1024], P('mem')
- key_grad: float32 [1024, 1024], P('mem')
- value_grad: float32 [1024, 1024], P('mem')
- out_grad: float32 [1024, 1024], P('mem')
- ffn_gain_grad: float32 [1024], P('mem')
- gate_grad: float32 [1024, 2816], P('mem')
- up_grad: float32 [1024, 2816], P('mem')
- down_grad: float32 [2816, 1024], P('mem')
Inputs may be any that keep to these rules, and one draw needn't show every extreme that they name: `padding_mask`: within each segment of 2048 consecutive tokens the ones form a prefix of 1024 tokens or more. `memory_length`: how many of a segment's 8192 memory slots are live. `chosen_keys`: row b belongs to the queries b * 512 to (b + 1) * 512 - 1; its first entry is below 2048.
All inputs are finite; a program needn't handle non-finite values.
Results may differ from a plain program's by a relative error of at most 0.014.
Values may be sent and summed in bfloat16 or wider, within the bound.
No kernel may reach another device: no remote copies, remote signals or barrier semaphores. Data moves between devices by JAX's collectives and lax.ppermute only.
A program may use at most 320 MiB of HBM per device.

v0:
```python
import math

import jax
import jax.numpy as jnp
from jax import lax
from jax.sharding import PartitionSpec as P

H = 8
HD = 128
SEG_LEN = 2048
QB = 512
TOPK = 128


EPSILON = 1e-05
NEGATIVE = -1e30


def outer_product(left, right):
    return lax.dot_general(
        left, right, (((0,), (0,)), ((), ())), preferred_element_type=jnp.float32
    )


def backward_dot(left, weight):
    return lax.dot_general(
        left, weight, (((1,), (1,)), ((), ())), preferred_element_type=jnp.float32
    )


def forward_dot(left, weight):
    return jnp.dot(left, weight, preferred_element_type=jnp.float32)


def normalize(values):
    factor = lax.rsqrt(jnp.mean(values * values, axis=-1, keepdims=True) + EPSILON)
    return (values * factor, factor)


def norm_back(grad_in, normed, factor, gain):
    scaled = grad_in * gain
    return factor * (scaled - normed * jnp.mean(scaled * normed, axis=-1, keepdims=True))


def block_stats(scores, usable):
    highest = jnp.max(scores, axis=-1)
    row_sum = jnp.sum(jnp.where(usable, jnp.exp(scores - highest[..., None]), 0.0), axis=-1)
    return (highest, row_sum)


def join_stats(high_left, sum_left, high_right, sum_right):
    highest = jnp.maximum(high_left, high_right)
    return (
        highest,
        sum_left * jnp.exp(high_left - highest) + sum_right * jnp.exp(high_right - highest),
    )


def local(
    tokens,
    padding_mask,
    memory_keys,
    memory_values,
    memory_length,
    chosen_keys,
    norm_gain,
    w_query,
    w_key,
    w_value,
    w_out,
    ffn_gain,
    w_gate,
    w_up,
    w_down,
    cotangent,
):
    group_size = lax.axis_size("mem")
    position = lax.axis_index("mem")
    tok_rows, model_width = tokens.shape
    memory_rows = memory_keys.shape[1]
    segment_count = memory_keys.shape[0]
    all_rows = tok_rows * group_size
    blocks = all_rows // QB
    segment_blocks = SEG_LEN // QB
    score_scale = 1.0 / math.sqrt(HD)
    inputs = tokens.astype(jnp.float32)
    normed_one, factor_one = normalize(inputs)
    h_one = (normed_one * norm_gain).astype(jnp.bfloat16)
    queries = forward_dot(h_one, w_query).astype(jnp.bfloat16)
    keyed_flat = forward_dot(h_one, w_key).astype(jnp.bfloat16)
    valued_flat = forward_dot(h_one, w_value).astype(jnp.bfloat16)
    own_keys = keyed_flat.reshape(tok_rows, H, HD)
    own_values = valued_flat.reshape(tok_rows, H, HD)
    first_row = position * tok_rows
    own_segment = first_row // SEG_LEN
    own_offset = first_row % SEG_LEN
    start_block = own_segment * segment_blocks
    key_position = own_offset + jnp.arange(tok_rows)
    key_usable = padding_mask == 1
    block_segment = jnp.arange(blocks) * QB // SEG_LEN
    segment_match = block_segment[:, None] == jnp.arange(segment_count)[None, :]
    limits = jnp.sum(jnp.where(segment_match, memory_length[None, :], 0), axis=1)
    shifted = chosen_keys - position * memory_rows
    owned = (shifted >= 0) & (shifted < memory_rows) & (chosen_keys < limits[:, None])
    columns = jnp.arange(memory_rows)

    def select_slots(pieces):
        local_rows, usable, segment = pieces
        table = ((local_rows[:, None] == columns[None, :]) & usable[:, None]).astype(jnp.bfloat16)
        keys_here = lax.dynamic_index_in_dim(memory_keys, segment, 0, keepdims=False)
        values_here = lax.dynamic_index_in_dim(memory_values, segment, 0, keepdims=False)
        return (
            forward_dot(table, keys_here).astype(jnp.bfloat16),
            forward_dot(table, values_here).astype(jnp.bfloat16),
        )

    picked_keys, picked_values = lax.map(select_slots, (shifted, owned, block_segment))
    gathered = lax.all_gather(queries, "mem", axis=0, tiled=True).reshape(blocks, QB, H, HD)
    picked_keys = picked_keys.reshape(blocks, TOPK, H, HD)
    picked_values = picked_values.reshape(blocks, TOPK, H, HD)

    def memory_scores(query_block, key_block, usable):
        scores = (
            jnp.einsum("qhd,thd->qht", query_block, key_block, preferred_element_type=jnp.float32)
            * score_scale
        )
        return jnp.where(usable[None, None, :], scores, NEGATIVE)

    def local_visible(block_index):
        query_position = block_index * QB + jnp.arange(QB)
        return (key_position[None, :] <= query_position[:, None]) & key_usable[None, :]

    def local_scores(query_block, visible):
        scores = (
            jnp.einsum("qhd,khd->qhk", query_block, own_keys, preferred_element_type=jnp.float32)
            * score_scale
        )
        return jnp.where(visible[:, None, :], scores, NEGATIVE)

    def segment_rows(source, block_index):
        return lax.dynamic_index_in_dim(source, start_block + block_index, 0, keepdims=False)

    def add_segment(whole, local_part):
        merged = lax.dynamic_slice_in_dim(whole, start_block, segment_blocks, 0) + local_part
        return lax.dynamic_update_slice_in_dim(whole, merged, start_block, 0)

    def memory_first(pieces):
        query_block, key_block, usable = pieces
        return block_stats(memory_scores(query_block, key_block, usable), usable[None, None, :])

    memory_high, memory_sum = lax.map(memory_first, (gathered, picked_keys, owned))

    def local_first(block_index):
        visible = local_visible(block_index)
        scores = local_scores(segment_rows(gathered, block_index), visible)
        return block_stats(scores, visible[:, None, :])

    local_high, local_sum = lax.map(local_first, jnp.arange(segment_blocks))
    seg_high = lax.dynamic_slice_in_dim(memory_high, start_block, segment_blocks, 0)
    seg_sum = lax.dynamic_slice_in_dim(memory_sum, start_block, segment_blocks, 0)
    seg_high, seg_sum = join_stats(seg_high, seg_sum, local_high, local_sum)
    memory_high = lax.dynamic_update_slice_in_dim(memory_high, seg_high, start_block, 0)
    memory_sum = lax.dynamic_update_slice_in_dim(memory_sum, seg_sum, start_block, 0)
    row_high = lax.pmax(memory_high.astype(jnp.bfloat16), "mem").astype(memory_high.dtype)
    row_sum = lax.psum(memory_sum * jnp.exp(memory_high - row_high), "mem")
    log_total = row_high + jnp.log(row_sum)

    def memory_second(pieces):
        query_block, key_block, value_block, usable, block_total = pieces
        scores = memory_scores(query_block, key_block, usable)
        weights = jnp.where(
            usable[None, None, :], jnp.exp(scores - block_total[..., None]), 0.0
        ).astype(jnp.bfloat16)
        return jnp.einsum("qht,thd->qhd", weights, value_block, preferred_element_type=jnp.float32)

    numerators = lax.map(memory_second, (gathered, picked_keys, picked_values, owned, log_total))

    def local_second(block_index):
        visible = local_visible(block_index)
        scores = local_scores(segment_rows(gathered, block_index), visible)
        block_total = segment_rows(log_total, block_index)
        weights = jnp.where(
            visible[:, None, :], jnp.exp(scores - block_total[..., None]), 0.0
        ).astype(jnp.bfloat16)
        return jnp.einsum("qhk,khd->qhd", weights, own_values, preferred_element_type=jnp.float32)

    numerators = add_segment(numerators, lax.map(local_second, jnp.arange(segment_blocks)))
    attended_sum = lax.psum_scatter(
        numerators.reshape(all_rows, model_width), "mem", scatter_dimension=0, tiled=True
    )
    attended = attended_sum.astype(jnp.bfloat16)
    residual = inputs + forward_dot(attended, w_out)
    normed_two, factor_two = normalize(residual)
    h_two = (normed_two * ffn_gain).astype(jnp.bfloat16)
    gate = forward_dot(h_two, w_gate)
    up_part = forward_dot(h_two, w_up)
    sigmoid_gate = jax.nn.sigmoid(gate)
    silu_gate = gate * sigmoid_gate
    act = (silu_gate * up_part).astype(jnp.bfloat16)
    mixed = (residual + forward_dot(act, w_down)).astype(jnp.bfloat16)
    down_grad = outer_product(act, cotangent)
    d_act = backward_dot(cotangent, w_down)
    d_gate = (d_act * up_part * sigmoid_gate * (1.0 + gate * (1.0 - sigmoid_gate))).astype(
        jnp.bfloat16
    )
    d_up = (d_act * silu_gate).astype(jnp.bfloat16)
    gate_grad = outer_product(h_two, d_gate)
    up_grad = outer_product(h_two, d_up)
    d_two = backward_dot(d_gate, w_gate) + backward_dot(d_up, w_up)
    ffn_gain_grad = jnp.sum(d_two * normed_two, axis=0)
    d_res = cotangent.astype(jnp.float32) + norm_back(d_two, normed_two, factor_two, ffn_gain)
    d_res_low = d_res.astype(jnp.bfloat16)
    out_grad = outer_product(attended, d_res_low)
    d_att = backward_dot(d_res_low, w_out).astype(jnp.bfloat16)
    grad_rows = lax.all_gather(d_att, "mem", axis=0, tiled=True).reshape(blocks, QB, H, HD)

    def memory_third(pieces):
        query_block, key_block, value_block, usable, block_total, grad_block = pieces
        scores = memory_scores(query_block, key_block, usable)
        probs = jnp.where(usable[None, None, :], jnp.exp(scores - block_total[..., None]), 0.0)
        pushes = jnp.einsum(
            "qhd,thd->qht", grad_block, value_block, preferred_element_type=jnp.float32
        )
        return jnp.sum(probs * pushes, axis=-1)

    delta_part = lax.map(
        memory_third, (gathered, picked_keys, picked_values, owned, log_total, grad_rows)
    )

    def local_third(block_index):
        visible = local_visible(block_index)
        scores = local_scores(segment_rows(gathered, block_index), visible)
        block_total = segment_rows(log_total, block_index)
        probs = jnp.where(visible[:, None, :], jnp.exp(scores - block_total[..., None]), 0.0)
        pushes = jnp.einsum(
            "qhd,khd->qhk",
            segment_rows(grad_rows, block_index),
            own_values,
            preferred_element_type=jnp.float32,
        )
        return jnp.sum(probs * pushes, axis=-1)

    delta_part = add_segment(delta_part, lax.map(local_third, jnp.arange(segment_blocks)))
    delta = lax.psum(delta_part, "mem")

    def memory_fourth(pieces):
        query_block, key_block, value_block, usable, block_total, grad_block, block_delta = pieces
        scores = memory_scores(query_block, key_block, usable)
        probs = jnp.where(usable[None, None, :], jnp.exp(scores - block_total[..., None]), 0.0)
        pushes = jnp.einsum(
            "qhd,thd->qht", grad_block, value_block, preferred_element_type=jnp.float32
        )
        d_scores = jnp.where(
            usable[None, None, :], probs * (pushes - block_delta[..., None]), 0.0
        ).astype(jnp.bfloat16)
        return (
            jnp.einsum("qht,thd->qhd", d_scores, key_block, preferred_element_type=jnp.float32)
            * score_scale
        )

    query_terms = lax.map(
        memory_fourth, (gathered, picked_keys, picked_values, owned, log_total, grad_rows, delta)
    )

    def local_fourth(running, block_index):
        key_acc, value_acc = running
        visible = local_visible(block_index)
        query_block = segment_rows(gathered, block_index)
        grad_block = segment_rows(grad_rows, block_index)
        scores = local_scores(query_block, visible)
        block_total = segment_rows(log_total, block_index)
        block_delta = segment_rows(delta, block_index)
        probs = jnp.where(visible[:, None, :], jnp.exp(scores - block_total[..., None]), 0.0)
        pushes = jnp.einsum(
            "qhd,khd->qhk", grad_block, own_values, preferred_element_type=jnp.float32
        )
        d_scores = jnp.where(
            visible[:, None, :], probs * (pushes - block_delta[..., None]), 0.0
        ).astype(jnp.bfloat16)
        query_term = (
            jnp.einsum("qhk,khd->qhd", d_scores, own_keys, preferred_element_type=jnp.float32)
            * score_scale
        )
        key_acc = (
            key_acc
            + jnp.einsum("qhk,qhd->khd", d_scores, query_block, preferred_element_type=jnp.float32)
            * score_scale
        )
        value_acc = value_acc + jnp.einsum(
            "qhk,qhd->khd",
            probs.astype(jnp.bfloat16),
            grad_block,
            preferred_element_type=jnp.float32,
        )
        return ((key_acc, value_acc), query_term)

    empty_acc = jnp.zeros((tok_rows, H, HD), jnp.float32)
    (key_sum, value_sum), local_terms = lax.scan(
        local_fourth, (empty_acc, empty_acc), jnp.arange(segment_blocks)
    )
    query_terms = add_segment(query_terms, local_terms)
    d_query = lax.psum_scatter(
        query_terms.reshape(all_rows, model_width), "mem", scatter_dimension=0, tiled=True
    ).astype(jnp.bfloat16)
    d_key = key_sum.reshape(tok_rows, model_width).astype(jnp.bfloat16)
    d_value = value_sum.reshape(tok_rows, model_width).astype(jnp.bfloat16)
    query_grad = outer_product(h_one, d_query)
    key_grad = outer_product(h_one, d_key)
    value_grad = outer_product(h_one, d_value)
    d_one = (
        backward_dot(d_query, w_query) + backward_dot(d_key, w_key) + backward_dot(d_value, w_value)
    )
    norm_gain_grad = jnp.sum(d_one * normed_one, axis=0)
    input_grad = (d_res + norm_back(d_one, normed_one, factor_one, norm_gain)).astype(jnp.bfloat16)
    shards = (
        lax.psum_scatter(norm_gain_grad, "mem", scatter_dimension=0, tiled=True),
        lax.psum_scatter(query_grad, "mem", scatter_dimension=0, tiled=True),
        lax.psum_scatter(key_grad, "mem", scatter_dimension=0, tiled=True),
        lax.psum_scatter(value_grad, "mem", scatter_dimension=0, tiled=True),
        lax.psum_scatter(out_grad, "mem", scatter_dimension=0, tiled=True),
        lax.psum_scatter(ffn_gain_grad, "mem", scatter_dimension=0, tiled=True),
        lax.psum_scatter(gate_grad, "mem", scatter_dimension=0, tiled=True),
        lax.psum_scatter(up_grad, "mem", scatter_dimension=0, tiled=True),
        lax.psum_scatter(down_grad, "mem", scatter_dimension=0, tiled=True),
    )
    (
        norm_part,
        query_part,
        key_part,
        value_part,
        out_part,
        ffn_gain_part,
        gate_part,
        up_grad_part,
        down_part,
    ) = shards
    summed = lax.psum(
        (
            norm_part,
            query_part,
            key_part,
            value_part,
            out_part,
            ffn_gain_part,
            gate_part,
            up_grad_part,
            down_part,
        ),
        "seg",
    )
    (
        norm_done,
        query_done,
        key_done,
        value_done,
        out_done,
        ffn_gain_done,
        gate_done,
        up_done,
        down_done,
    ) = summed
    return (
        mixed,
        input_grad,
        norm_done,
        query_done,
        key_done,
        value_done,
        out_done,
        ffn_gain_done,
        gate_done,
        up_done,
        down_done,
    )


def solution(mesh):
    return jax.shard_map(
        local,
        mesh=mesh,
        in_specs=(
            P(("seg", "mem"), None),
            P(("seg", "mem")),
            P("seg", "mem", None),
            P("seg", "mem", None),
            P("seg"),
            P("seg", None),
            P(),
            P(),
            P(),
            P(),
            P(),
            P(),
            P(),
            P(),
            P(),
            P(("seg", "mem"), None),
        ),
        out_specs=(
            P(("seg", "mem"), None),
            P(("seg", "mem"), None),
            P("mem"),
            P("mem", None),
            P("mem", None),
            P("mem", None),
            P("mem", None),
            P("mem"),
            P("mem", None),
            P("mem", None),
            P("mem", None),
        ),
        check_vma=False,
    )
```

profile of v0, /device:TPU:0, one launch (start us, length us, event | category | flops | bytes accessed | tf_op | source)
XLA Modules:
  0.0 1458.7 jit_solution(2463133091801142676)
XLA Ops:
  15.4 22.5 %while.110 = (s32[]{:T(128)}, bf16[4,128,1024]{2,1,0:T(8,128)(2,1)}, bf16[4,128,1024]{2,1,0:T(8,128)(2,1)}, s32[4,128]{1,0:T(4,128)S(1)}, pred[4,128]{1,0:T(4,12...) while((s32[]{:T(128)}, bf16[4,128,1024]{2,1,0:T(8,128)(2,1)}, ...), condition=%wide.region_2.3_spmd.clone, body=%wide.region_1.2_spmd.clone.sunk | while | flops 537657344 | bytes 4721261 | solution.py:117
  57.8 20.9 %while.111 = (s32[]{:T(128)}, f32[4,512,8]{1,2,0:T(8,128)S(1)}, f32[4,512,8]{1,2,0:T(8,128)S(1)}, s32[4]{0:T(128)S(1)}, pred[256]{0:T(512)(128)(4,1)S(1)}, /*ind...) while((s32[]{:T(128)}, f32[4,512,8]{1,2,0:T(8,128)S(1)}, ...), condition=%wide.region_10.11_spmd.clone, body=%wide.region_7.10_spmd.clone.sunk | while | flops 277078784 | bytes 10475995 | solution.py:158
  88.6 23.5 %pmax.7 = bf16[4,512,8]{1,2,0:T(8,128)(2,1)S(1)} all-reduce(bf16[4,512,8]{1,2,0:T(8,128)(2,1)S(1)} %get-tuple-element.1010), channel_id=1, replica_groups=mesh['seg'=4,'mem'=8] {'mem'}, use_global_device_ids=true, to_apply=%region_11.12 | all-reduce | flops 16384 | bytes 65536 | tf_op jit(solution)/shard_map/pmax | solution.py:164
  119.1 46.3 %all-reduce.9.cloned.1.call-done = f32[4,512,8]{1,2,0:T(8,128)} async-done(((f32[4,512,8]{1,2,0:T(8,128)}), f32[4,512,8]{1,2,0:T(8,128)}) %all-reduce.9.cloned.1.call-update) | async-done | bytes 65552 | tf_op jit(solution)/shard_map/psum | solution.py:165
  170.5 26.2 %while.112 = (s32[]{:T(128)}, f32[4,512,8,128]{3,1,2,0:T(8,128)}, s32[4]{0:T(128)S(1)}, pred[256]{0:T(512)(128)(4,1)S(1)}, s32[]{:T(128)}, /*index=5*/bf16[4,512...) while((s32[]{:T(128)}, f32[4,512,8,128]{3,1,2,0:T(8,128)}, ...), condition=%wide.region_16.17_spmd.clone, body=%wide.region_15.16_spmd.clone.sunk | while | flops 542376704 | bytes 4643303 | solution.py:187
  201.0 46.6 %while.107 = (s32[]{:T(128)}, f32[4,512,8,128]{3,1,2,0:T(8,128)}, bf16[4,128,8,128]{3,2,1,0:T(8,128)(2,1)}, pred[4,128]{1,0:T(4,128)(4,1)S(1)}, bf16[4,128,8,128...) while((s32[]{:T(128)}, f32[4,512,8,128]{3,1,2,0:T(8,128)}, ...), condition=%wide.region_14.15_spmd, body=%wide.region_13.14_spmd.sunk | while | flops 271056896 | bytes 13158765 | solution.py:176
  271.5 70.8 %reduce-scatter.10.cloned.1.call-done = f32[256,1024]{1,0:T(8,128)} async-done(((f32[2048,1024]{1,0:T(8,128)}), f32[256,1024]{1,0:T(8,128)}) %reduce-scatter.10.cloned.1.call-update) | async-done | bytes 1048592 | tf_op jit(solution)/shard_map/reduce_scatter | solution.py:188
  370.4 34.3 %all-gather.5.cloned.1.call-done = bf16[2048,1024]{1,0:T(8,128)(2,1)} async-done(((bf16[256,1024]{1,0:T(8,128)(2,1)}), bf16[2048,1024]{1,0:T(8,128)(2,1)}) %all-gather.5.cloned.1.call-update) | async-done | bytes 4194320 | tf_op jit(solution)/shard_map/all_gather | solution.py:215
  410.9 28.1 %while.113 = (s32[]{:T(128)}, f32[4,512,8]{1,2,0:T(8,128)S(1)}, s32[4]{0:T(128)S(1)}, pred[256]{0:T(512)(128)(4,1)S(1)}, s32[]{:T(128)}, /*index=5*/bf16[4,512,8...) while((s32[]{:T(128)}, f32[4,512,8]{1,2,0:T(8,128)S(1)}, ...), condition=%wide.region_25.26_spmd.clone, body=%wide.region_23.25_spmd.clone.sunk | while | flops 543421184 | bytes 12032499 | solution.py:243
  439.0 15.7 %while.108 = (s32[]{:T(128)}, f32[4,512,8]{1,2,0:T(8,128)S(1)}, pred[4,128]{1,0:T(4,128)(4,1)S(1)}, bf16[4,128,8,128]{3,1,2,0:T(8,128)(2,1)}, bf16[4,512,8,128]{...) while((s32[]{:T(128)}, f32[4,512,8]{1,2,0:T(8,128)S(1)}, ...), condition=%wide.region_22.23_spmd, body=%wide.region_20.22_spmd.sunk | while | flops 271577088 | bytes 6917489 | solution.py:226
  455.5 52.6 %all-reduce.11.cloned.1.call-done = f32[4,512,8]{1,2,0:T(8,128)} async-done(((f32[4,512,8]{1,2,0:T(8,128)}), f32[4,512,8]{1,2,0:T(8,128)}) %all-reduce.11.cloned.1.call-update) | async-done | bytes 65552 | tf_op jit(solution)/shard_map/psum | solution.py:244
  512.3 55.4 %while.109 = (s32[]{:T(128)}, f32[4,512,8,128]{3,1,2,0:T(8,128)}, bf16[4,128,8,128]{3,1,2,0:T(8,128)(2,1)}, pred[4,128]{1,0:T(4,128)(4,1)S(1)}, bf16[4,512,8,128...) while((s32[]{:T(128)}, f32[4,512,8,128]{3,1,2,0:T(8,128)}, ...), condition=%wide.region_28.29_spmd, body=%wide.region_27.28_spmd.sunk | while | flops 407371776 | bytes 17665912 | solution.py:261
  571.9 50.7 %while.114 = (s32[]{:T(128)}, f32[256,8,128]{0,2,1:T(8,128)}, f32[256,8,128]{0,2,1:T(8,128)}, f32[4,512,8,128]{3,1,2,0:T(8,128)}, s32[4]{0:T(128)S(1)}, /*index=...) while((s32[]{:T(128)}, f32[256,8,128]{0,2,1:T(8,128)}, ...), condition=%wide.region_30.31_spmd.clone, body=%wide.region_29.30_spmd.clone.sunk | while | flops 1357906688 | bytes 65264296 | solution.py:298
  684.4 33.0 %reduce-scatter.12.cloned.1.call-done = f32[256,1024]{1,0:T(8,128)} async-done(((f32[2048,1024]{1,0:T(8,128)}), f32[256,1024]{1,0:T(8,128)}) %reduce-scatter.12.cloned.1.call-update) | async-done | bytes 1048592 | tf_op jit(solution)/shard_map/reduce_scatter | solution.py:302
  721.5 50.6 %reduce-scatter.20.cloned.1.call-done = f32[128,1024]{1,0:T(8,128)} async-done(((f32[1024,1024]{1,0:T(8,128)}), f32[128,1024]{1,0:T(8,128)}) %reduce-scatter.20.cloned.1.call-update) | async-done | bytes 524304 | tf_op jit(solution)/shard_map/reduce_scatter | solution.py:320
  772.1 55.1 %reduce-scatter.18.cloned.1.call-done = f32[128,1024]{1,0:T(8,128)} async-done(((f32[1024,1024]{1,0:T(8,128)}), f32[128,1024]{1,0:T(8,128)}) %reduce-scatter.18.cloned.1.call-update) | async-done | bytes 524304 | tf_op jit(solution)/shard_map/reduce_scatter | solution.py:319
  827.2 54.7 %reduce-scatter.16.cloned.1.call-done = f32[128,1024]{1,0:T(8,128)} async-done(((f32[1024,1024]{1,0:T(8,128)}), f32[128,1024]{1,0:T(8,128)}) %reduce-scatter.16.cloned.1.call-update) | async-done | bytes 524304 | tf_op jit(solution)/shard_map/reduce_scatter | solution.py:318
  881.9 90.6 %reduce-scatter.24.cloned.1.call-done = f32[128,2816]{1,0:T(8,128)} async-done(((f32[1024,2816]{1,0:T(8,128)}), f32[128,2816]{1,0:T(8,128)}) %reduce-scatter.24.cloned.1.call-update) | async-done | bytes 1441808 | tf_op jit(solution)/shard_map/reduce_scatter | solution.py:323
  972.4 90.7 %reduce-scatter.22.cloned.1.call-done = f32[128,2816]{1,0:T(8,128)} async-done(((f32[1024,2816]{1,0:T(8,128)}), f32[128,2816]{1,0:T(8,128)}) %reduce-scatter.22.cloned.1.call-update) | async-done | bytes 1441808 | tf_op jit(solution)/shard_map/reduce_scatter | solution.py:322
  1063.1 90.5 %reduce-scatter.26.cloned.1.call-done = f32[352,1024]{1,0:T(8,128)} async-done(((f32[2816,1024]{1,0:T(8,128)}), f32[352,1024]{1,0:T(8,128)}) %reduce-scatter.26.cloned.1.call-update) | async-done | bytes 1441808 | tf_op jit(solution)/shard_map/reduce_scatter | solution.py:324
  1153.7 55.0 %reduce-scatter.14.cloned.1.call-done = f32[128,1024]{1,0:T(8,128)} async-done(((f32[1024,1024]{1,0:T(8,128)}), f32[128,1024]{1,0:T(8,128)}) %reduce-scatter.14.cloned.1.call-update) | async-done | bytes 524304 | tf_op jit(solution)/shard_map/reduce_scatter | solution.py:317
  1221.0 13.1 all-reduce.2
  1234.3 12.5 all-reduce.3
  1249.5 191.5 %all-reduce.13.cloned.1.call-done = (f32[128,1024]{1,0:T(8,128)}, f32[128,1024]{1,0:T(8,128)}, f32[128,1024]{1,0:T(8,128)}, f32[128,1024]{1,0:T(8,128)}, f32[128...) async-done(((f32[128,1024]{1,0:T(8,128)}, f32[128,1024]{1,0:T(8,128)}, f32[128,1024]{1,0:T(8,128)}, f32[128,1024]{1,0:T(8,128)}, f32[128,2816]{1,0:T(8,128)}, ...) | async-done | bytes 6422544 | tf_op jit(solution)/shard_map/psum | solution.py:337
  (453 shorter events, 464.4 us)
Async XLA Ops:
  7.2 106.0 %copy-start = (bf16[1024,1024]{1,0:T(8,128)(2,1)S(1)}, bf16[1024,1024]{1,0:T(8,128)(2,1)}, u32[]{:S(2)}) copy-start(bf16[1024,1024]{1,0:T(8,128)(2,1)} %param.43) | copy-start | bytes 6291460
  7.2 44.4 %all-gather.3.cloned.1.call-start = ((), (), s32[]{:S(2)}) async-start(), calls=%async_computation.9 | async-start | bytes 4718592 | tf_op jit(solution)/shard_map/all_gather | solution.py:118
  8.6 104.5 %copy-start.27 = (f32[256]{0:T(256)}, f32[256]{0:T(256)S(1)}, u32[]{:S(2)}) copy-start(f32[256]{0:T(256)S(1)} %add_rsqrt_fusion.1) | copy-start | bytes 3076
  12.1 153.4 %all-reduce.9.cloned.1.call-start = ((), (), s32[]{:S(2)}) async-start(), calls=%async_computation.10 | async-start | bytes 131072 | tf_op jit(solution)/shard_map/psum | solution.py:165
  112.8 229.5 %reduce-scatter.10.cloned.1.call-start = ((), (), s32[]{:S(2)}) async-start(), calls=%async_computation.11 | async-start | bytes 9437184 | tf_op jit(solution)/shard_map/reduce_scatter | solution.py:188
  271.5 73.7 %copy-start.29 = (f32[1024]{0:T(1024)S(1)}, f32[1024]{0:T(1024)}, u32[]{:S(2)}) copy-start(f32[1024]{0:T(1024)} %param.45) | copy-start | bytes 12292
  271.5 133.3 %all-gather.5.cloned.1.call-start = ((), (), s32[]{:S(2)}) async-start(), calls=%async_computation.12 | async-start | bytes 4718592 | tf_op jit(solution)/shard_map/all_gather | solution.py:215
  342.3 9.4 slice-start
  345.1 19.9 %copy-start.6 = (f32[256,1024]{1,0:T(8,128)}, f32[256,1024]{1,0:T(8,128)S(1)}, u32[]{:S(2)}) copy-start(f32[256,1024]{1,0:T(8,128)S(1)} %get-tuple-element.1028) | copy-start | bytes 3145732
  345.4 9.6 slice-start.4
  351.7 10.9 slice-start.2
  367.9 140.2 %all-reduce.11.cloned.1.call-start = ((), (), s32[]{:S(2)}) async-start(), calls=%async_computation.13 | async-start | bytes 131072 | tf_op jit(solution)/shard_map/psum | solution.py:244
  455.4 261.9 %reduce-scatter.12.cloned.1.call-start = ((), (), s32[]{:S(2)}) async-start(), calls=%async_computation.14 | async-start | bytes 9437184 | tf_op jit(solution)/shard_map/reduce_scatter | solution.py:302
  646.5 125.5 %reduce-scatter.20.cloned.1.call-start = ((), (), s32[]{:S(2)}) async-start(), calls=%async_computation.18 | async-start | bytes 4718592 | tf_op jit(solution)/shard_map/reduce_scatter | solution.py:320
  651.0 176.2 %reduce-scatter.18.cloned.1.call-start = ((), (), s32[]{:S(2)}) async-start(), calls=%async_computation.17 | async-start | bytes 4718592 | tf_op jit(solution)/shard_map/reduce_scatter | solution.py:319
  655.9 226.0 %reduce-scatter.16.cloned.1.call-start = ((), (), s32[]{:S(2)}) async-start(), calls=%async_computation.16 | async-start | bytes 4718592 | tf_op jit(solution)/shard_map/reduce_scatter | solution.py:318
  661.2 311.2 %reduce-scatter.24.cloned.1.call-start = ((), (), s32[]{:S(2)}) async-start(), calls=%async_computation.20 | async-start | bytes 12976128 | tf_op jit(solution)/shard_map/reduce_scatter | solution.py:323
  669.1 394.0 %reduce-scatter.22.cloned.1.call-start = ((), (), s32[]{:S(2)}) async-start(), calls=%async_computation.19 | async-start | bytes 12976128 | tf_op jit(solution)/shard_map/reduce_scatter | solution.py:322
  676.7 477.0 %reduce-scatter.26.cloned.1.call-start = ((), (), s32[]{:S(2)}) async-start(), calls=%async_computation.21 | async-start | bytes 12976128 | tf_op jit(solution)/shard_map/reduce_scatter | solution.py:324
  684.3 524.4 %reduce-scatter.14.cloned.1.call-start = ((), (), s32[]{:S(2)}) async-start(), calls=%async_computation.15 | async-start | bytes 4718592 | tf_op jit(solution)/shard_map/reduce_scatter | solution.py:317
  721.4 487.3 %copy-start.33 = (u32[32]{0:T(128)S(1)}, u32[32]{0:T(128)}, u32[]{:S(2)}) copy-start(u32[32]{0:T(128)} %constant.261) | copy-start | bytes 388
  721.4 719.5 %all-reduce.13.cloned.1.call-start = ((), (), s32[]{:S(2)}) async-start(), calls=%async_computation.22 | async-start | bytes 12845056 | tf_op jit(solution)/shard_map/psum | solution.py:337
  1440.9 8.9 copy-start.19
  1443.0 8.0 copy-start.18
  (45 other events, 145.0 us)
Sparse Core Ops, SparseCore 0:
  12.2 39.4 all-gather.2
  112.9 52.4 all-reduce.8
  271.6 70.6 reduce-scatter.9
  368.0 36.7 all-gather.4
  455.5 52.4 all-reduce.10
  646.7 70.6 reduce-scatter.11
  720.7 51.3 reduce-scatter.19
  775.8 51.3 reduce-scatter.17
  830.5 51.2 reduce-scatter.15
  885.6 86.7 reduce-scatter.23
  976.3 86.7 reduce-scatter.21
  1066.9 86.7 reduce-scatter.25
  1157.4 51.2 reduce-scatter.13
  1211.5 229.3 all-reduce.12
where the time goes:
time: 1470 us; the launch traced here: 1460 us
  waiting for transfers between devices  927 us (63%)
  matrix products  254 us (17%)
  local copies, waits for them, and re-layouts  149 us (10%)
  blocking collectives  49.1 us (3%)
  other arithmetic  39.6 us (3%)
  loops' own time  23.4 us (2%)
  between operations  16.1 us (1%)
    psum x1, waiting for transfers between devices, local(): lax.psum((norm_part, query_part, key_part, value_part, out_part, ffn_gain...  191 us
    reduce_scatter x1, waiting for transfers between devices, local(): lax.psum_scatter(gate_grad, 'mem', scatter_dimension=0, tiled=True)  90.7 us
    reduce_scatter x1, waiting for transfers between devices, local(): lax.psum_scatter(up_grad, 'mem', scatter_dimension=0, tiled=True)  90.6 us
    reduce_scatter x1, waiting for transfers between devices, local(): lax.psum_scatter(down_grad, 'mem', scatter_dimension=0, tiled=True)  90.5 us
    reduce_scatter x1, waiting for transfers between devices, local(): lax.psum_scatter(numerators.reshape(all_rows, model_width), 'mem', scatte...  70.8 us
    reduce_scatter x1, waiting for transfers between devices, local(): lax.psum_scatter(value_grad, 'mem', scatter_dimension=0, tiled=True)  55.1 us
    reduce_scatter x1, waiting for transfers between devices, local(): lax.psum_scatter(query_grad, 'mem', scatter_dimension=0, tiled=True)  55 us
    reduce_scatter x1, waiting for transfers between devices, local(): lax.psum_scatter(key_grad, 'mem', scatter_dimension=0, tiled=True)  54.7 us
  transfers between devices with their start and end apart: 14, of which 14 were waited for; matrix products, arithmetic and copies ran while one was open for 6% of the time, Pallas kernels for 0%

commit v1 on v0

v1 whole, which is shorter than its diff:
```python
import math

import jax
import jax.numpy as jnp
import numpy as np
from jax import lax
from jax.experimental import pallas as pl
from jax.experimental.pallas import tpu as pltpu
from jax.sharding import PartitionSpec as P

H = 8
HD = 128
SEG_LEN = 2048
QB = 512
TOPK = 128
EPSILON = 1e-05
NEGATIVE = -1e30
SCALE = 1.0 / math.sqrt(HD)
SCALE2 = SCALE / math.log(2.0)
TEAM = 8
EXTRA = 16
F32 = jnp.float32
BF16 = jnp.bfloat16
ORDER_EVEN = np.array([0, 2, 4, 6, 1, 5, 3, 7], np.int32)
ORDER_ODD = np.array([0, 4, 2, 6, 1, 3, 5, 7], np.int32)
NN = (((1,), (0,)), ((), ()))
NT = (((1,), (1,)), ((), ()))
TN = (((0,), (0,)), ((), ()))
VMEM_LIMIT = 60 * 1024 * 1024


def dot(left, right, dims=NN):
    return lax.dot_general(left, right, dims, preferred_element_type=F32)


def mixed(even_step, odd_step):
    size = lax.axis_size("mem")
    return [(i, i ^ (even_step if i % 2 == 0 else odd_step)) for i in range(size)]


def partner():
    return mixed(1, 1)


def gather_team(block):
    block = jnp.concatenate([block, lax.ppermute(block, "mem", mixed(2, 4))], axis=0)
    block = jnp.concatenate([block, lax.ppermute(block, "mem", mixed(4, 2))], axis=0)
    return jnp.concatenate([block, lax.ppermute(block, "mem", partner())], axis=0)


def scatter_sum_team(blocks):
    kept = blocks[:4] + lax.ppermute(blocks[4:], "mem", partner())
    kept = kept[:2] + lax.ppermute(kept[2:], "mem", mixed(4, 2))
    return kept[0] + lax.ppermute(kept[1], "mem", mixed(2, 4))


def swap_team(blocks):
    near = jnp.stack([blocks[0], blocks[2], blocks[4], blocks[5]])
    far = jnp.stack([blocks[1], blocks[3], blocks[6], blocks[7]])
    far = lax.ppermute(far, "mem", mixed(2, 4))
    both = jnp.stack([near, far], axis=1)
    got = lax.ppermute(both[1::2], "mem", mixed(4, 2))
    both = jnp.concatenate([both[0::2], got], axis=1)
    got = lax.ppermute(both[1], "mem", partner())
    return jnp.concatenate([both[0], got], axis=0)


def merge_teams(pieces):
    teams = lax.axis_size("mem") // TEAM
    if teams == 1:
        return pieces[0]
    mine = lax.axis_index("mem") // TEAM
    total = lax.dynamic_index_in_dim(pieces, mine, 0, keepdims=False)
    for step in range(1, teams):
        there = (mine + step) % teams
        piece = lax.dynamic_index_in_dim(pieces, there, 0, keepdims=False)
        perm = [
            (t * TEAM + s, (t + step) % teams * TEAM + s) for t in range(teams) for s in range(TEAM)
        ]
        total = total + lax.ppermute(piece, "mem", perm)
    return total


def line_sum(part):
    count = lax.axis_size("seg")
    if count == 1:
        return part
    index = lax.axis_index("seg")
    half = count // 2
    for k in range(half - 1):
        part = part + lax.ppermute(part, "seg", [(k, k + 1), (count - 1 - k, count - 2 - k)])
    part = part + lax.ppermute(part, "seg", [(half - 1, half), (half, half - 1)])
    for k in reversed(range(half - 1)):
        got = lax.ppermute(part, "seg", [(k + 1, k), (count - 2 - k, count - 1 - k)])
        part = jnp.where((index == k) | (index == count - 1 - k), got, part)
    return part


def params():
    return pltpu.CompilerParams(vmem_limit_bytes=VMEM_LIMIT)


def whole():
    return pl.BlockSpec(memory_space=pltpu.VMEM)


def pick_kernel(order, rows, counts, keys, values, out, table):
    @pl.when(pl.program_id(1) == 0)
    def _():
        slots = lax.broadcasted_iota(jnp.int32, table.shape, 1)
        table[...] = jnp.where(rows[...] == slots, 1.0, 0.0).astype(BF16)

    out[0, 0, : table.shape[0], :HD] = dot(table[...], keys[0]).astype(BF16)
    out[0, 0, : table.shape[0], HD:] = dot(table[...], values[0]).astype(BF16)
    lane = lax.broadcasted_iota(jnp.int32, (EXTRA, 2 * HD), 1)
    full, rest = counts[pl.program_id(0), 0], counts[pl.program_id(0), 1]
    tail = jnp.where(lane == 0, full, jnp.where(lane == 1, rest, 0))
    out[0, 0, table.shape[0] :, :] = tail.astype(F32).astype(BF16)


def pick(order, rows, counts, keys, values):
    segments, depth, width = keys.shape
    slots = rows.shape[0] // segments
    block = pl.BlockSpec((1, depth, HD), lambda g, j, order, counts: (g, 0, order[j]))

    def body(order, counts, rows, keys, values, out, table):
        pick_kernel(order, rows, counts, keys, values, out, table)

    return pl.pallas_call(
        body,
        out_shape=jax.ShapeDtypeStruct((segments, TEAM, slots + EXTRA, 2 * HD), BF16),
        grid_spec=pltpu.PrefetchScalarGridSpec(
            num_scalar_prefetch=2,
            grid=(segments, TEAM),
            in_specs=[
                pl.BlockSpec((slots, 1), lambda g, j, order, counts: (g, 0)),
                block,
                block,
            ],
            out_specs=pl.BlockSpec(
                (1, 1, slots + EXTRA, 2 * HD), lambda g, j, order, counts: (g, j, 0, 0)
            ),
            scratch_shapes=[pltpu.VMEM((slots, depth), BF16)],
        ),
        compiler_params=params(),
        name="pick_memory",
    )(order, counts, rows, keys, values)


def project_kernel(order, x, gain, wq, wk, wv, h, q, k, v, w):
    @pl.when(pl.program_id(0) == 0)
    def _():
        w[:, :HD] = wq[...]
        w[:, HD : 2 * HD] = wk[...]
        w[:, 2 * HD :] = wv[...]

    values = x[...].astype(F32)
    factor = lax.rsqrt(jnp.mean(values * values, axis=-1, keepdims=True) + EPSILON)
    low = (values * factor * gain[...]).astype(BF16)
    h[...] = low
    made = dot(low, w[...]).astype(BF16)
    q[...] = made[:, :HD]
    k[...] = made[:, HD : 2 * HD]
    v[...] = made[:, 2 * HD :]


def project(order, x, gain, w_query, w_key, w_value):
    total, width = x.shape
    rows = total // TEAM
    column = pl.BlockSpec((width, HD), lambda j, order: (0, order[0]))
    head = pl.BlockSpec((rows, HD), lambda j, order: (order[j], 0))
    flat = pl.BlockSpec((rows, width), lambda j, order: (j, 0))
    return pl.pallas_call(
        project_kernel,
        out_shape=[jax.ShapeDtypeStruct((total, width), BF16)]
        + [jax.ShapeDtypeStruct((total, HD), BF16)] * 3,
        grid_spec=pltpu.PrefetchScalarGridSpec(
            num_scalar_prefetch=1,
            grid=(TEAM,),
            in_specs=[flat, pl.BlockSpec((1, width), lambda j, order: (0, 0))] + [column] * 3,
            out_specs=[flat, head, head, head],
            scratch_shapes=[pltpu.VMEM((width, 3 * HD), BF16)],
        ),
        compiler_params=params(),
        name="project",
    )(order, x, gain, w_query, w_key, w_value)


def attend_kernel(q, k, v, memory, usable, out, out_full, lse):
    slots = usable.shape[0] * usable.shape[1]
    real = memory[slots : slots + 1, 0:1].astype(F32) * 256.0 + memory[slots : slots + 1, 1:2].astype(F32)
    step = 256
    for b in range(SEG_LEN // step):
        seen = (b + 1) * step
        block = b * step // QB
        queries = q[b * step : (b + 1) * step, :]
        scores = dot(queries, k[:seen, :], NT) * SCALE2
        row = lax.broadcasted_iota(jnp.int32, scores.shape, 0) + b * step
        column = lax.broadcasted_iota(jnp.int32, scores.shape, 1)
        live = (column <= row) & (column.astype(F32) < real)
        scores = jnp.where(live, scores, NEGATIVE)
        far = dot(queries, memory[block * TOPK : (block + 1) * TOPK, :HD], NT) * SCALE2
        far = jnp.where(usable[block : block + 1, :] > 0, far, NEGATIVE)
        top = jnp.maximum(
            jnp.max(scores, axis=1, keepdims=True), jnp.max(far, axis=1, keepdims=True)
        )
        near_weight = jnp.exp2(scores - top)
        far_weight = jnp.exp2(far - top)
        total = jnp.sum(near_weight, axis=1, keepdims=True) + jnp.sum(
            far_weight, axis=1, keepdims=True
        )
        sums = dot(near_weight.astype(BF16), v[:seen, :]) + dot(
            far_weight.astype(BF16), memory[block * TOPK : (block + 1) * TOPK, HD:]
        )
        sums = sums / total
        out_full[b * step : (b + 1) * step, :] = sums
        out[b * step : (b + 1) * step, :] = sums.astype(BF16)
        log_total = jnp.broadcast_to(top + jnp.log2(total), (step, HD))
        lse[:, b * step : (b + 1) * step] = jnp.transpose(log_total)[:8, :]


def attend(q, k, v, memory, usable):
    total = q.shape[0]
    return pl.pallas_call(
        attend_kernel,
        out_shape=[
            jax.ShapeDtypeStruct((total, HD), BF16),
            jax.ShapeDtypeStruct((total, HD), F32),
            jax.ShapeDtypeStruct((8, total), F32),
        ],
        in_specs=[whole()] * 5,
        out_specs=[whole()] * 3,
        compiler_params=params(),
        name="attend",
    )(q, k, v, memory, usable)


def attend_back_kernel(
    order, q, k, v, memory, usable, lse, full, grads, out, d_res, d_out, delta, dq, dk, dv
):
    slots = usable.shape[0]
    real = memory[slots : slots + 1, 0:1].astype(F32) * 256.0 + memory[slots : slots + 1, 1:2].astype(F32)
    rows = grads.shape[1]
    for j in range(TEAM):
        start = pl.multiple_of(order[j] * rows, rows)
        piece = grads[j, :, :HD]
        d_out[pl.ds(start, rows), :] = piece
        d_res[pl.ds(start, rows), :] = grads[j, :, HD:]
        dots = piece.astype(F32) * full[pl.ds(start, rows), :]
        delta[:, pl.ds(start, rows)] = jnp.broadcast_to(
            jnp.sum(jnp.transpose(dots), axis=0, keepdims=True), (8, rows)
        )
    dq[...] = jnp.zeros_like(dq)
    dk[...] = jnp.zeros_like(dk)
    dv[...] = jnp.zeros_like(dv)

    def tile(i, j, diagonal):
        at_q = pl.ds(pl.multiple_of(i * QB, QB), QB)
        at_k = pl.ds(pl.multiple_of(j * QB, QB), QB)
        queries, keys, grad = q[at_q, :], k[at_k, :], d_out[at_q, :]
        position = lax.broadcasted_iota(jnp.int32, (QB, 1), 0) + j * QB
        bias = jnp.where(position.astype(F32) < real, 0.0, NEGATIVE)
        scores = dot(keys, queries, NT) * SCALE2 - lse[0:1, at_q] + bias
        if diagonal:
            row = lax.broadcasted_iota(jnp.int32, (QB, QB), 0)
            column = lax.broadcasted_iota(jnp.int32, (QB, QB), 1)
            scores = jnp.where(row <= column, scores, NEGATIVE)
        weight = jnp.exp2(scores)
        push = dot(v[at_k, :], grad, NT)
        d_score = (weight * (push - delta[0:1, at_q])).astype(BF16)
        dv[at_k, :] += dot(weight.astype(BF16), grad)
        dk[at_k, :] += dot(d_score, queries)
        dq[at_q, :] += dot(d_score, keys, TN)

    def far_tile(i):
        at_q = pl.ds(pl.multiple_of(i * QB, QB), QB)
        at_m = pl.ds(pl.multiple_of(i * TOPK, TOPK), TOPK)
        keys = memory[at_m, :HD]
        bias = jnp.where(usable[at_m, :] > 0, 0.0, NEGATIVE)
        scores = dot(keys, q[at_q, :], NT) * SCALE2 - lse[0:1, at_q] + bias
        weight = jnp.exp2(scores)
        push = dot(memory[at_m, HD:], d_out[at_q, :], NT)
        d_score = (weight * (push - delta[0:1, at_q])).astype(BF16)
        dq[at_q, :] += dot(d_score, keys, TN)

    def outer(i, carry):
        tile(i, i, True)
        far_tile(i)

        def inner(j, carry):
            tile(i, j, False)
            return carry

        return lax.fori_loop(0, i, inner, carry)

    lax.fori_loop(0, SEG_LEN // QB, outer, 0)
    for j in range(TEAM):
        at = pl.ds(pl.multiple_of(order[j] * rows, rows), rows)
        out[j, :, :HD] = (dq[at, :] * SCALE).astype(BF16)
        out[j, :, HD : 2 * HD] = (dk[at, :] * SCALE).astype(BF16)
        out[j, :, 2 * HD :] = dv[at, :].astype(BF16)


def attend_back(order, q, k, v, memory, usable, lse, full, grads):
    total = q.shape[0]
    rows = total // TEAM
    return pl.pallas_call(
        attend_back_kernel,
        out_shape=[
            jax.ShapeDtypeStruct((TEAM, rows, 3 * HD), BF16),
            jax.ShapeDtypeStruct((total, HD), BF16),
        ],
        in_specs=[pl.BlockSpec(memory_space=pltpu.SMEM)] + [whole()] * 8,
        out_specs=[whole()] * 2,
        scratch_shapes=[
            pltpu.VMEM((total, HD), BF16),
            pltpu.VMEM((8, total), F32),
            pltpu.VMEM((total, HD), F32),
            pltpu.VMEM((total, HD), F32),
            pltpu.VMEM((total, HD), F32),
        ],
        compiler_params=params(),
        name="attend_back",
    )(order, q, k, v, memory, usable, lse, full, grads)


def residual_kernel(order, heads, x, w_out, gain, h, own, w):
    @pl.when(pl.program_id(0) == 0)
    def _():
        for j in range(TEAM):
            start = pl.multiple_of(order[j] * HD, HD)
            w[j * HD : (j + 1) * HD, :] = w_out[pl.ds(start, HD), :]

    attended = jnp.concatenate([heads[j] for j in range(TEAM)], axis=1)
    residual = x[...].astype(F32) + dot(attended, w[...])

    @pl.when(pl.program_id(0) == 0)
    def _():
        own[...] = residual

    factor = lax.rsqrt(jnp.mean(residual * residual, axis=-1, keepdims=True) + EPSILON)
    h[...] = (residual * factor * gain[...]).astype(BF16)


def residual_all(order, heads, x, w_out, gain):
    total, width = x.shape
    rows = total // TEAM
    flat = pl.BlockSpec((rows, width), lambda j, order: (j, 0))
    return pl.pallas_call(
        residual_kernel,
        out_shape=[
            jax.ShapeDtypeStruct((total, width), BF16),
            jax.ShapeDtypeStruct((rows, width), F32),
        ],
        grid_spec=pltpu.PrefetchScalarGridSpec(
            num_scalar_prefetch=1,
            grid=(TEAM,),
            in_specs=[
                pl.BlockSpec((TEAM, rows, HD), lambda j, order: (0, order[j], 0)),
                flat,
                pl.BlockSpec((width, width), lambda j, order: (0, 0)),
                pl.BlockSpec((1, width), lambda j, order: (0, 0)),
            ],
            out_specs=[flat, pl.BlockSpec((rows, width), lambda j, order: (0, 0))],
            scratch_shapes=[pltpu.VMEM((width, width), BF16)],
        ),
        compiler_params=params(),
        name="residual_all",
    )(order, heads, x, w_out, gain)


def input_grad_kernel(order, grads, x, gain, d_res, wq, wk, wv, out, acc):
    step = pl.program_id(0)
    w = jnp.concatenate([wq[...], wk[...], wv[...]], axis=1)
    part = dot(grads[0], w, NT)

    @pl.when(step == 0)
    def _():
        acc[...] = part

    @pl.when(step > 0)
    def _():
        acc[...] += part

    @pl.when(step == TEAM - 1)
    def _():
        values = x[...].astype(F32)
        factor = lax.rsqrt(jnp.mean(values * values, axis=-1, keepdims=True) + EPSILON)
        normed = values * factor
        scaled = acc[...] * gain[...]
        mean = jnp.mean(scaled * normed, axis=-1, keepdims=True)
        out[...] = (d_res[...] + factor * (scaled - normed * mean)).astype(BF16)


def input_grad_of(order, grads, x, gain, d_res, w_query, w_key, w_value):
    rows, width = x.shape
    column = pl.BlockSpec((width, HD), lambda j, order: (0, order[j]))
    fixed = pl.BlockSpec((rows, width), lambda j, order: (0, 0))
    return pl.pallas_call(
        input_grad_kernel,
        out_shape=jax.ShapeDtypeStruct((rows, width), BF16),
        grid_spec=pltpu.PrefetchScalarGridSpec(
            num_scalar_prefetch=1,
            grid=(TEAM,),
            in_specs=[
                pl.BlockSpec((1, rows, 3 * HD), lambda j, order: (j, 0, 0)),
                fixed,
                pl.BlockSpec((1, width), lambda j, order: (0, 0)),
                fixed,
                column,
                column,
                column,
            ],
            out_specs=fixed,
            scratch_shapes=[pltpu.VMEM((rows, width), F32)],
        ),
        compiler_params=params(),
        name="input_grad",
    )(order, grads, x, gain, d_res, w_query, w_key, w_value)


def in_order(blocks, places):
    return jnp.concatenate(
        [lax.dynamic_index_in_dim(blocks, places[j], 0, keepdims=True) for j in range(TEAM)], axis=0
    )


def columns_in_order(values, order):
    rows = values.shape[0]
    return jnp.stack(
        [lax.dynamic_slice(values, (0, order[j] * HD), (rows, HD)) for j in range(TEAM)]
    )


def to_owners(part):
    teams = lax.axis_size("mem") // TEAM
    if teams == 1:
        return part
    rows = part.shape[0] // teams
    mine = merge_teams(part.reshape(teams, rows, part.shape[1]))
    perm = [(t * TEAM + s, s * teams + t) for t in range(teams) for s in range(TEAM)]
    return lax.ppermute(mine, "mem", perm)


def local(
    tokens,
    padding_mask,
    memory_keys,
    memory_values,
    memory_length,
    chosen_keys,
    norm_gain,
    w_query,
    w_key,
    w_value,
    w_out,
    ffn_gain,
    w_gate,
    w_up,
    w_down,
    cotangent,
):
    place = lax.axis_index("mem")
    members = lax.axis_size("mem")
    team, member = place // TEAM, place % TEAM
    rows, width = tokens.shape
    hidden = w_gate.shape[1]
    share = hidden // TEAM
    segments, memory_rows = memory_keys.shape[0], memory_keys.shape[1]
    blocks = SEG_LEN // QB
    slots = blocks * TOPK
    order = member ^ jnp.where(member % 2 == 0, ORDER_EVEN, ORDER_ODD)
    where = jnp.zeros((TEAM,), jnp.int32)
    where = jnp.sum(
        jnp.where(order[None, :] == jnp.arange(TEAM)[:, None], jnp.arange(TEAM)[None, :], 0), axis=1
    ).astype(jnp.int32)
    gain_one, gain_two = norm_gain.reshape(1, width), ffn_gain.reshape(1, width)

    x_all = gather_team(tokens)
    chosen = chosen_keys.reshape(segments, slots)
    live = chosen < memory_length[:, None]
    shifted = chosen - place * memory_rows
    owned = live & (shifted >= 0) & (shifted < memory_rows)
    picked_rows = jnp.where(owned, shifted, -1).reshape(segments * slots, 1)
    count = jnp.sum(padding_mask)
    full = count == rows
    counts = jnp.where(
        jnp.arange(segments)[:, None] == team,
        jnp.stack([full.astype(jnp.int32), jnp.where(full, 0, count).astype(jnp.int32)])[None, :],
        0,
    )
    picked = pick(order, picked_rows, counts, memory_keys, memory_values)
    memory = scatter_sum_team(merge_teams(picked))
    own_live = lax.dynamic_index_in_dim(live, team, 0, keepdims=False).astype(jnp.int32)

    h_one, query, keyed, valued = project(order, x_all, gain_one, w_query, w_key, w_value)
    attended, attended_full, lse = attend(
        query, keyed, valued, memory, own_live.reshape(blocks, TOPK)
    )
    heads = gather_team(attended.reshape(1, SEG_LEN, HD))
    cot_all = gather_team(cotangent)
    h_two, residual = residual_all(order, heads, x_all, w_out, gain_two)

    own_h = h_two[:rows]
    gate = dot(own_h, w_gate)
    up = dot(own_h, w_up)
    d_act = dot(cotangent, w_down, NT)
    sigmoid = jax.nn.sigmoid(gate)
    silu = gate * sigmoid
    act = (silu * up).astype(BF16)
    d_gate = (d_act * up * sigmoid * (1.0 + gate * (1.0 - sigmoid))).astype(BF16)
    d_up = (d_act * silu).astype(BF16)
    d_two = dot(d_gate, w_gate, NT) + dot(d_up, w_up, NT)
    factor_two = lax.rsqrt(jnp.mean(residual * residual, axis=-1, keepdims=True) + EPSILON)
    normed_two = residual * factor_two
    scaled = d_two * gain_two
    d_res = cotangent.astype(F32) + factor_two * (
        scaled - normed_two * jnp.mean(scaled * normed_two, axis=-1, keepdims=True)
    )
    d_low = d_res.astype(BF16)
    d_att = dot(d_low, w_out, NT).astype(BF16)
    mixed_out = (residual + dot(act, w_down)).astype(BF16)
    grads = swap_team(
        jnp.concatenate([columns_in_order(d_att, order), columns_in_order(d_low, order)], axis=2)
    )

    gate_cols = lax.dynamic_slice(w_gate, (0, member * share), (width, share))
    up_cols = lax.dynamic_slice(w_up, (0, member * share), (width, share))
    down_rows = lax.dynamic_slice(w_down, (member * share, 0), (share, width))
    gate_all = dot(h_two, gate_cols)
    up_all = dot(h_two, up_cols)
    d_act_all = dot(cot_all, down_rows, NT)
    sigmoid_all = jax.nn.sigmoid(gate_all)
    silu_all = gate_all * sigmoid_all
    act_all = (silu_all * up_all).astype(BF16)
    d_gate_all = (
        d_act_all * up_all * sigmoid_all * (1.0 + gate_all * (1.0 - sigmoid_all))
    ).astype(BF16)
    d_up_all = (d_act_all * silu_all).astype(BF16)
    down_part = dot(act_all, cot_all, TN).astype(BF16)
    gate_part = dot(d_gate_all, h_two, TN).astype(BF16)
    up_part = dot(d_up_all, h_two, TN).astype(BF16)
    down_done = line_sum(to_owners(down_part)).astype(F32)

    def hidden_grad(part):
        got = in_order(swap_team(columns_in_order(part, order)), where)
        return line_sum(to_owners(jnp.transpose(got.reshape(hidden, HD))))

    gate_done = hidden_grad(gate_part).astype(F32)
    up_done = hidden_grad(up_part).astype(F32)

    d_heads, d_low_cols = attend_back(
        order, query, keyed, valued, memory, own_live.reshape(slots, 1), lse, attended_full, grads
    )
    flat = d_heads.reshape(SEG_LEN, 3 * HD)
    square = columns_in_order(dot(flat, h_one, TN).astype(BF16), order)
    out_part = jnp.stack([dot(d_low_cols, heads[j], TN) for j in range(TEAM)]).astype(BF16)
    square = in_order(swap_team(jnp.concatenate([square, out_part], axis=1)), where)
    square = square.reshape(TEAM, 4, HD, HD)
    done = [
        line_sum(to_owners(jnp.transpose(square[:, n].reshape(width, HD)))).astype(F32)
        for n in range(4)
    ]
    query_done, key_done, value_done, out_done = done

    input_grad = input_grad_of(
        order, swap_team(d_heads), tokens, gain_one, d_res, w_query, w_key, w_value
    )

    out_rows = width // members

    def own_rows(weight):
        return lax.dynamic_slice(weight, (place * out_rows, 0), (out_rows, weight.shape[1])).astype(F32)

    def own_gain(gain):
        return lax.dynamic_slice(gain, (place * out_rows,), (out_rows,))

    norm_done = (
        jnp.sum(own_rows(w_query) * query_done, axis=1)
        + jnp.sum(own_rows(w_key) * key_done, axis=1)
        + jnp.sum(own_rows(w_value) * value_done, axis=1)
    ) / own_gain(norm_gain)
    ffn_done = (
        jnp.sum(own_rows(w_gate) * gate_done, axis=1) + jnp.sum(own_rows(w_up) * up_done, axis=1)
    ) / own_gain(ffn_gain)
    return (
        mixed_out,
        input_grad,
        norm_done,
        query_done,
        key_done,
        value_done,
        out_done,
        ffn_done,
        gate_done,
        up_done,
        down_done,
    )


def solution(mesh):
    return jax.shard_map(
        local,
        mesh=mesh,
        in_specs=(
            P(("seg", "mem"), None),
            P(("seg", "mem")),
            P("seg", "mem", None),
            P("seg", "mem", None),
            P("seg"),
            P("seg", None),
            P(),
            P(),
            P(),
            P(),
            P(),
            P(),
            P(),
            P(),
            P(),
            P(("seg", "mem"), None),
        ),
        out_specs=(
            P(("seg", "mem"), None),
            P(("seg", "mem"), None),
            P("mem"),
            P("mem", None),
            P("mem", None),
            P("mem", None),
            P("mem", None),
            P("mem"),
            P("mem", None),
            P("mem", None),
            P("mem", None),
        ),
        check_vma=False,
    )
```

time: 1470 us -> 409 us (0.28)
  waiting for transfers between devices: 927 us -> 86.2 us
  matrix products: 254 us -> 54.3 us
  local copies, waits for them, and re-layouts: 149 us -> 31.6 us
  starting transfers between devices: 1.05 us -> 78.5 us
  Pallas kernels: 0 us -> 65.7 us
  blocking collectives: 49.1 us -> 0 us
  other arithmetic: 39.6 us -> 63 us
  loops' own time: 23.4 us -> 0 us
    reduce_scatter x9 -> x0, waiting for transfers between devices: 591 us -> none  [the longest x1 90.7 us: local(): lax.psum_scatter(gate_grad, 'mem', scatter_dimension=0, tiled=True)]
    psum x3 -> x0, waiting for transfers between devices: 290 us -> none  [the longest x1 191 us: local(): lax.psum((norm_part, query_part, key_part, value_part, out_part, ffn_gain...]
    dot_general x89 -> x22, matrix products: 254 us -> 54.3 us  [dot(): return lax.dot_general(left, right, dims, preferred_element_type=F32)]
    ppermute x0 -> x48, waiting for transfers between devices: none -> 86.2 us  [the longest x3 22.7 us: gather_team(): lax.ppermute(block, 'mem', mixed(4, 2))]
    ppermute x0 -> x48, starting transfers between devices: none -> 78.5 us  [the longest x7 40.4 us: line_sum(): lax.ppermute(part, 'seg', [(k, k + 1), (count - 1 - k, count - 2 - k)])]
    pallas_call x0 -> x6, Pallas kernels: none -> 65.7 us  [the longest x1 14.6 us: attend_back(): pl.pallas_call(attend_back_kernel, out_shape=[jax.ShapeDtypeStruct((TEAM,...]
    dynamic_update_slice x32 -> x0, local copies, waits for them, and re-layouts: 48.1 us -> none  [the longest x16 48 us: local(): lax.map(memory_second, (gathered, picked_keys, picked_values, owned, log_...]
    all_gather x2 -> x0, waiting for transfers between devices: 45.5 us -> none  [the longest x1 34.3 us: local(): lax.all_gather(d_att, 'mem', axis=0, tiled=True).reshape(blocks, QB, H, HD)]
  transfers between devices with their start and end apart: 14 -> 48, of which waited for: 14 -> 16; matrix products, arithmetic and copies ran while one was open for 6% -> 27% of each run, Pallas kernels for 0% -> 13%
where the time goes in v1:
time: 409 us; the launch traced here: 404 us
  waiting for transfers between devices  86.2 us (21%)
  starting transfers between devices  78.5 us (19%)
  Pallas kernels  65.7 us (16%)
  other arithmetic  63 us (15%)
  matrix products  54.3 us (13%)
  local copies, waits for them, and re-layouts  31.6 us (8%)
  between operations  24.3 us (6%)
    dot_general x22, matrix products, dot(): return lax.dot_general(left, right, dims, preferred_element_type=F32)  54.3 us
    ppermute x7, starting transfers between devices, line_sum(): lax.ppermute(part, 'seg', [(k, k + 1), (count - 1 - k, count - 2 - k)])  40.4 us
    ppermute x3, waiting for transfers between devices, gather_team(): lax.ppermute(block, 'mem', mixed(4, 2))  22.7 us
    pallas_call x1, Pallas kernels, attend_back(): pl.pallas_call(attend_back_kernel, out_shape=[jax.ShapeDtypeStruct((TEAM,...  14.6 us
    ppermute x5, waiting for transfers between devices, swap_team(): far = lax.ppermute(far, 'mem', mixed(2, 4))  14 us
    pallas_call x1, Pallas kernels, residual_all(): pl.pallas_call(residual_kernel, out_shape=[jax.ShapeDtypeStruct((total, w...  13.3 us
    ppermute x3, waiting for transfers between devices, gather_team(): lax.ppermute(block, 'mem', mixed(2, 4))  13 us
    ppermute x1, waiting for transfers between devices, scatter_sum_team(): kept = kept[:2] + lax.ppermute(kept[2:], 'mem', mixed(4, 2))  12.5 us
  transfers between devices with their start and end apart: 48, of which 16 were waited for; matrix products, arithmetic and copies ran while one was open for 27% of the time, Pallas kernels for 13%

profile of v1, /device:TPU:0, one launch (start us, length us, event | category | flops | bytes accessed | tf_op | source)
XLA Modules:
  0.0 403.6 jit_solution(1272574406138307726)
XLA Ops:
  11.8 10.1 %pick_memory.1 = bf16[1,8,528,256]{3,2,1,0:T(8,128)(2,1)} custom-call(s32[8]{0:T(128)} %fusion.124.order, s32[1,2]{1,0:T(1,128)} %broadcast_select_fusion.counts, s32[512,1]{1,0:T(8,128)} %and_select_fusion.rows, bf16[1,1024,1024]{2,1,0:T(8,128)(2,1)} %keys.1, bf16[1,1024,1024]{2,1,0:T(8,128)(2,1)} %values.1), custom_call_target="tpu_custom_call" | custom-call | tf_op jit(solution)/shard_map/pick_memory/pallas_call | solution.py:129
  24.9 11.9 %collective-permute-done.1 = bf16[512,1024]{1,0:T(8,128)(2,1)S(1)} collective-permute-done((bf16[512,1024]{1,0:T(8,128)(2,1)S(1)}, bf16[512,1024]{1,0:T(8,128)(2,1)S(1)}, u32[]{:S(2)}, u32[]{:S(2)}) %collective-permute-start.1) | collective-permute-done | bytes 1048608 | tf_op jit(solution)/shard_map/ppermute | solution.py:47
  39.5 12.5 %collective-permute-done.4 = bf16[2,528,256]{2,1,0:T(8,128)(2,1)S(1)} collective-permute-done((bf16[2,528,256]{2,1,0:T(8,128)(2,1)S(1)}, bf16[2,528,256]{2,1,0:T(8,128)(2,1)S(1)}, u32[]{:S(2)}, u32[]{:S(2)}) %collective-permute-start.4) | collective-permute-done | bytes 540704 | tf_op jit(solution)/shard_map/ppermute | solution.py:53
  55.0 3.7 collective-permute-done.5
  60.9 9.4 %project.1 = (bf16[2048,1024]{1,0:T(8,128)(2,1)}, bf16[2048,128]{1,0:T(8,128)(2,1)}, bf16[2048,128]{1,0:T(8,128)(2,1)}, bf16[2048,128]{1,0:T(8,128)(2,1)}) custom-call(s32[8]{0:T(128)} %fusion.124.order, bf16[2048,1024]{1,0:T(8,128)(2,1)} %constant_dynamic-update-slice_fusion.x, f32[1,1024]{1,0:T(1,128)} %bitcast.284, bf16[1024,1024]{1,0:T(8,128)(2,1)} %wq.3, ...), custom_call_target="tpu_custom_call" | custom-call | tf_op jit(solution)/shard_map/project/pallas_call | solution.py:173
  70.3 7.9 %attend.1 = (bf16[2048,128]{1,0:T(8,128)(2,1)}, f32[2048,128]{1,0:T(8,128)}, f32[8,2048]{1,0:T(8,128)}) custom-call(bf16[2048,128]{1,0:T(8,128)(2,1)} %get-tuple-element.22.q, bf16[2048,128]{1,0:T(8,128)(2,1)} %get-tuple-element.23.k, bf16[2048,128]{1,0:T(8,128)(2,1)} %get-tuple-element.24.v, bf16[528,256]{1,0:T(8,128)(2,1)} %fusion.90.memory, ...), custom_call_target="tpu_custom_call" | custom-call | tf_op jit(solution)/shard_map/attend/pallas_call | solution.py:224
  80.3 13.0 %collective-permute-done.6 = bf16[1,2048,128]{2,1,0:T(8,128)(2,1)S(1)} collective-permute-done((bf16[1,2048,128]{2,1,0:T(8,128)(2,1)}, bf16[1,2048,128]{2,1,0:T(8,128)(2,1)S(1)}, u32[]{:S(2)}, u32[]{:S(2)}) %collective-permute-start.6) | collective-permute-done | bytes 524320 | tf_op jit(solution)/shard_map/ppermute | solution.py:46
  98.5 10.8 %collective-permute-done.7 = bf16[2,2048,128]{2,1,0:T(8,128)(2,1)S(1)} collective-permute-done((bf16[2,2048,128]{2,1,0:T(8,128)(2,1)S(1)}, bf16[2,2048,128]{2,1,0:T(8,128)(2,1)S(1)}, u32[]{:S(2)}, u32[]{:S(2)}) %collective-permute-start.7) | collective-permute-done | bytes 1048608 | tf_op jit(solution)/shard_map/ppermute | solution.py:47
  119.6 5.9 %fusion.144 = f32[256,2816]{1,0:T(8,128)} fusion(bf16[256,1024]{1,0:T(8,128)(2,1)S(1)} %copy-done.3, bf16[2816,1024]{1,0:T(8,128)(2,1)} %param.32), kind=kOutput, calls=%fused_computation.379 | convolution fusion | flops 1476395008 | bytes 9175040 | tf_op jit(solution)/shard_map/dot_general | solution.py:33
  127.4 5.2 %fusion.53 = f32[2048,352]{0,1:T(8,128)} fusion(bf16[2048,1024]{1,0:T(8,128)(2,1)S(1)} %constant_dynamic-update-slice_fusion.36, bf16[2816,1024]{1,0:T(8,128)(2,1)} %param.32, s32[]{:T(128)S(6)} %select_n.234), kind=kOutput, calls=%fused_computation.176 | convolution fusion | flops 1476395008 | bytes 7798788 | tf_op jit(solution)/shard_map/dot_general | solution.py:33
  136.1 13.3 %residual_all.1 = (bf16[2048,1024]{1,0:T(8,128)(2,1)}, f32[256,1024]{1,0:T(8,128)}) custom-call(s32[8]{0:T(128)} %fusion.124.order, bf16[8,2048,128]{2,1,0:T(8,128)(2,1)} %pad_maximum_fusion.heads, bf16[2048,1024]{1,0:T(8,128)(2,1)} %constant_dynamic-update-slice_fusion.x, bf16[1024,1024]{1,0:T(8,128)(2,1)} %w_out.1, f32[1,1024]{1,0:T(1,128)} %bitcast.287), custom_call_target="tpu_custom_call" | custom-call | tf_op jit(solution)/shard_map/residual_all/pallas_call | solution.py:349
  149.4 4.6 %fusion.82 = f32[256,2816]{1,0:T(8,128)S(1)} fusion(bf16[1024,2816]{1,0:T(8,128)(2,1)} %param.30, bf16[2048,1024]{1,0:T(8,128)(2,1)} %get-tuple-element.27), kind=kOutput, calls=%fused_computation.213 | convolution fusion | flops 1476395008 | bytes 9175040 | tf_op jit(solution)/shard_map/dot_general | solution.py:33
  154.1 6.9 %fusion.80 = f32[256,2816]{1,0:T(8,128)} fusion(bf16[1024,2816]{1,0:T(8,128)(2,1)} %param.31, bf16[2048,1024]{1,0:T(8,128)(2,1)S(1)} %copy-done.23), kind=kOutput, calls=%fused_computation.211 | convolution fusion | flops 1476395008 | bytes 9175040 | tf_op jit(solution)/shard_map/dot_general | solution.py:33
  163.1 4.8 %multiply_reduce_fusion.2 = (f32[256]{0:T(256)S(1)}, f32[256,1024]{1,0:T(8,128)S(1)}) fusion(f32[256,1024]{1,0:T(8,128)S(1)} %copy-done.4, f32[256]{0:T(256)S(1)} %add_rsqrt_fusion, f32[1024]{0:T(1024)S(1)} %copy-done.22, f32[256,1024]{1,0:T(8,128)S(1)} %fusion.3, bf16[1024,2816]{1,0:T(8,128)(2,1)S(1)} %bitcast.281, f32[256,2816]{1,0:T(8,128)} %copy-done.26, ...), kind=kOutput, calls=%fused_computation.149 | convolution fusion | flops 1484914432 | bytes 17569792 | tf_op jit(solution)/shard_map/dot_general | solution.py:33
  184.9 4.8 %collective-permute-start.45 = (bf16[352,1024]{1,0:T(8,128)(2,1)}, bf16[352,1024]{1,0:T(8,128)(2,1)}, u32[]{:S(2)}, u32[]{:S(2)}) collective-permute-start(bf16[352,1024]{1,0:T(8,128)(2,1)} %fusion.9), channel_id=1, source_target_pairs={{0,8},{24,16},{1,9},{25,17},{2,10},{26,18},{3,11},{27,19},{4,12},{... | collective-permute-start | bytes 2162696 | tf_op jit(solution)/shard_map/ppermute | solution.py:91
  189.8 5.4 %collective-permute-done.33 = bf16[4,352,128]{2,1,0:T(8,128)(2,1)S(1)} collective-permute-done((bf16[4,352,128]{2,1,0:T(8,128)(2,1)S(1)}, bf16[4,352,128]{2,1,0:T(8,128)(2,1)S(1)}, u32[]{:S(2)}, u32[]{:S(2)}) %collective-permute-start.33) | collective-permute-done | bytes 360480 | tf_op jit(solution)/shard_map/ppermute | solution.py:60
  237.6 7.2 %collective-permute-start.36 = (bf16[128,2816]{0,1:T(8,128)(2,1)}, bf16[128,2816]{0,1:T(8,128)(2,1)}, u32[]{:S(2)}, u32[]{:S(2)}) collective-permute-start(bf16[128,2816]{0,1:T(8,128)(2,1)} %bitcast.103), channel_id=1, source_target_pairs={{0,8},{24,16},{1,9},{25,17},{2,10},{26,18},{3,11},{27,19},{4,12},{... | collective-permute-start | bytes 2162696 | tf_op jit(solution)/shard_map/ppermute | solution.py:91
  255.1 14.6 %attend_back.1 = (bf16[8,256,384]{2,1,0:T(8,128)(2,1)}, bf16[2048,128]{1,0:T(8,128)(2,1)}) custom-call(s32[8]{0:T(128)} %fusion.124.order, bf16[2048,128]{1,0:T(8,128)(2,1)} %get-tuple-element.22.q, bf16[2048,128]{1,0:T(8,128)(2,1)} %get-tuple-element.23.k, bf16[2048,128]{1,0:T(8,128)(2,1)} %get-tuple-element.24.v, bf16[528,256]{1,0:T(8,128)(2,1)} %fusion.90.memory, ...), custom_call_target="tpu_custom_call" | custom-call | tf_op jit(solution)/shard_map/attend_back/pallas_call | solution.py:307
  273.3 4.1 %convolution_convert_fusion = bf16[384,1024]{1,0:T(8,128)(2,1)S(1)} fusion(bf16[2048,384]{1,0:T(8,128)(2,1)S(1)} %bitcast.267, bf16[2048,1024]{1,0:T(8,128)(2,1)} %get-tuple-element.31), kind=kOutput, calls=%fused_computation.49 | convolution fusion | flops 1611005952 | bytes 6553600 | tf_op jit(solution)/shard_map/dot_general | solution.py:33
  288.6 5.4 %collective-permute-done.15 = bf16[4,512,128]{2,1,0:T(8,128)(2,1)S(1)} collective-permute-done((bf16[4,512,128]{2,1,0:T(8,128)(2,1)S(1)}, bf16[4,512,128]{2,1,0:T(8,128)(2,1)S(1)}, u32[]{:S(2)}, u32[]{:S(2)}) %collective-permute-start.15) | collective-permute-done | bytes 524320 | tf_op jit(solution)/shard_map/ppermute | solution.py:60
  299.1 4.3 %collective-permute-done.16 = bf16[2,2,512,128]{3,2,1,0:T(8,128)(2,1)S(1)} collective-permute-done((bf16[2,2,512,128]{3,2,1,0:T(8,128)(2,1)S(1)}, bf16[2,2,512,128]{3,2,1,0:T(8,128)(2,1)S(1)}, u32[]{:S(2)}, u32[]{:S(2)}) %collective-permute-start.16) | collective-permute-done | bytes 524320 | tf_op jit(solution)/shard_map/ppermute | solution.py:62
  315.9 19.2 %collective-permute-start.24 = (bf16[128,1024]{1,0:T(8,128)(2,1)S(1)}, bf16[128,1024]{1,0:T(8,128)(2,1)}, u32[]{:S(2)}, u32[]{:S(2)}) collective-permute-start(bf16[128,1024]{1,0:T(8,128)(2,1)S(1)} %bitcast.270), channel_id=1, source_target_pairs={{0,8},{24,16},{1,9},{25,17},{2,10},{26,18},{3,11},{27,19},{4,12},{... | collective-permute-start | bytes 786440 | tf_op jit(solution)/shard_map/ppermute | solution.py:91
  348.5 3.9 collective-permute-done.21
  390.8 10.5 %input_grad.1 = bf16[256,1024]{1,0:T(8,128)(2,1)} custom-call(s32[8]{0:T(128)} %fusion.124.order, bf16[8,256,384]{2,1,0:T(8,128)(2,1)} %pad_maximum_fusion.5.grads, bf16[256,1024]{1,0:T(8,128)(2,1)} %x.1, f32[1,1024]{1,0:T(1,128)} %bitcast.285, f32[256,1024]{1,0:T(8,128)} %get-tuple-element.77.d_res, bf16[1024,1024]{1,0:T(8,128)(2,1)} %wq.3, ...), custom_call_target="tpu_custom_call" | custom-call | tf_op jit(solution)/shard_map/input_grad/pallas_call | solution.py:399
  (324 shorter events, 180.0 us)
Async XLA Ops:
  0.6 21.2 %collective-permute-start = (bf16[256,1024]{1,0:T(8,128)(2,1)}, bf16[256,1024]{1,0:T(8,128)(2,1)S(1)}, u32[]{:S(2)}, u32[]{:S(2)}) collective-permute-start(bf16[256,1024]{1,0:T(8,128)(2,1)} %x.1), channel_id=1, source_target_pairs={{0,2},{1,5},{2,0},{3,7},{4,6},{5,1},{6,4},{7,3},{8,10},{9,13},{10,... | collective-permute-start | bytes 1572872 | tf_op jit(solution)/shard_map/ppermute | solution.py:46
  37.1 22.3 %collective-permute-start.2 = (bf16[1024,1024]{1,0:T(8,128)(2,1)S(1)}, bf16[1024,1024]{1,0:T(8,128)(2,1)S(1)}, u32[]{:S(2)}, u32[]{:S(2)}) collective-permute-start(bf16[1024,1024]{1,0:T(8,128)(2,1)S(1)} %pad_maximum_fusion.1), channel_id=1, source_target_pairs={{0,1},{1,0},{2,3},{3,2},{4,5},{5,4},{6,7},{7,6},{8,9},{9,8},{10,11... | collective-permute-start | bytes 6291464 | tf_op jit(solution)/shard_map/ppermute | solution.py:48
  39.0 39.2 %collective-permute-start.30 = (bf16[256,1024]{1,0:T(8,128)(2,1)S(1)}, bf16[256,1024]{1,0:T(8,128)(2,1)S(1)}, u32[]{:S(2)}, u32[]{:S(2)}) collective-permute-start(bf16[256,1024]{1,0:T(8,128)(2,1)S(1)} %copy-done.3), channel_id=1, source_target_pairs={{0,2},{1,5},{2,0},{3,7},{4,6},{5,1},{6,4},{7,3},{8,10},{9,13},{10,... | collective-permute-start | bytes 1572872 | tf_op jit(solution)/shard_map/ppermute | solution.py:46
  78.3 17.9 %collective-permute-start.31 = (bf16[512,1024]{1,0:T(8,128)(2,1)S(1)}, bf16[512,1024]{1,0:T(8,128)(2,1)S(1)}, u32[]{:S(2)}, u32[]{:S(2)}) collective-permute-start(bf16[512,1024]{1,0:T(8,128)(2,1)S(1)} %pad_maximum_fusion.11), channel_id=1, source_target_pairs={{0,4},{1,3},{2,6},{3,1},{4,0},{5,7},{6,2},{7,5},{8,12},{9,11},{10,... | collective-permute-start | bytes 3145736 | tf_op jit(solution)/shard_map/ppermute | solution.py:47
  97.7 27.9 %collective-permute-start.32 = (bf16[1024,1024]{1,0:T(8,128)(2,1)}, bf16[1024,1024]{1,0:T(8,128)(2,1)}, u32[]{:S(2)}, u32[]{:S(2)}) collective-permute-start(bf16[1024,1024]{1,0:T(8,128)(2,1)} %pad_maximum_fusion.3), channel_id=1, source_target_pairs={{0,1},{1,0},{2,3},{3,2},{4,5},{5,4},{6,7},{7,6},{8,9},{9,8},{10,11... | collective-permute-start | bytes 6291464 | tf_op jit(solution)/shard_map/ppermute | solution.py:48
  111.8 20.8 %collective-permute-start.8 = (bf16[4,2048,128]{2,1,0:T(8,128)(2,1)}, bf16[4,2048,128]{2,1,0:T(8,128)(2,1)}, u32[]{:S(2)}, u32[]{:S(2)}) collective-permute-start(bf16[4,2048,128]{2,1,0:T(8,128)(2,1)} %pad_maximum_fusion.2), channel_id=1, source_target_pairs={{0,1},{1,0},{2,3},{3,2},{4,5},{5,4},{6,7},{7,6},{8,9},{9,8},{10,11... | collective-permute-start | bytes 6291464 | tf_op jit(solution)/shard_map/ppermute | solution.py:48
  182.1 21.1 %collective-permute-start.9 = (bf16[4,256,256]{2,1,0:T(8,128)(2,1)S(1)}, bf16[4,256,256]{2,1,0:T(8,128)(2,1)S(1)}, u32[]{:S(2)}, u32[]{:S(2)}) collective-permute-start(bf16[4,256,256]{2,1,0:T(8,128)(2,1)S(1)} %get-tuple-element.107), channel_id=1, source_target_pairs={{0,2},{1,5},{2,0},{3,7},{4,6},{5,1},{6,4},{7,3},{8,10},{9,13},{10,... | collective-permute-start | bytes 1572872 | tf_op jit(solution)/shard_map/ppermute | solution.py:60
  184.9 43.8 %collective-permute-start.45 = (bf16[352,1024]{1,0:T(8,128)(2,1)}, bf16[352,1024]{1,0:T(8,128)(2,1)}, u32[]{:S(2)}, u32[]{:S(2)}) collective-permute-start(bf16[352,1024]{1,0:T(8,128)(2,1)} %fusion.9), channel_id=1, source_target_pairs={{0,8},{24,16},{1,9},{25,17},{2,10},{26,18},{3,11},{27,19},{4,12},{... | collective-permute-start | bytes 2162696 | tf_op jit(solution)/shard_map/ppermute | solution.py:91
  201.4 25.4 %collective-permute-start.40 = (bf16[2,2,352,128]{3,2,1,0:T(8,128)(2,1)}, bf16[2,2,352,128]{3,2,1,0:T(8,128)(2,1)}, u32[]{:S(2)}, u32[]{:S(2)}) collective-permute-start(bf16[2,2,352,128]{3,2,1,0:T(8,128)(2,1)} %get-tuple-element.113), channel_id=1, source_target_pairs={{0,4},{1,3},{2,6},{3,1},{4,0},{5,7},{6,2},{7,5},{8,12},{9,11},{10,... | collective-permute-start | bytes 1081352 | tf_op jit(solution)/shard_map/ppermute | solution.py:62
  204.4 26.6 %collective-permute-start.10 = (bf16[2,2,256,256]{3,2,1,0:T(8,128)(2,1)}, bf16[2,2,256,256]{3,2,1,0:T(8,128)(2,1)}, u32[]{:S(2)}, u32[]{:S(2)}) collective-permute-start(bf16[2,2,256,256]{3,2,1,0:T(8,128)(2,1)} %get-tuple-element.105), channel_id=1, source_target_pairs={{0,4},{1,3},{2,6},{3,1},{4,0},{5,7},{6,2},{7,5},{8,12},{9,11},{10,... | collective-permute-start | bytes 1572872 | tf_op jit(solution)/shard_map/ppermute | solution.py:62
  206.4 25.8 %collective-permute-start.35 = (bf16[4,352,128]{2,1,0:T(8,128)(2,1)}, bf16[4,352,128]{2,1,0:T(8,128)(2,1)S(1)}, u32[]{:S(2)}, u32[]{:S(2)}) collective-permute-start(bf16[4,352,128]{2,1,0:T(8,128)(2,1)} %get-tuple-element.123), channel_id=1, source_target_pairs={{0,1},{1,0},{2,3},{3,2},{4,5},{5,4},{6,7},{7,6},{8,9},{9,8},{10,11... | collective-permute-start | bytes 1081352 | tf_op jit(solution)/shard_map/ppermute | solution.py:64
  228.1 16.8 %collective-permute-start.41 = (bf16[4,352,128]{2,1,0:T(8,128)(2,1)S(1)}, bf16[4,352,128]{2,1,0:T(8,128)(2,1)S(1)}, u32[]{:S(2)}, u32[]{:S(2)}) collective-permute-start(bf16[4,352,128]{2,1,0:T(8,128)(2,1)S(1)} %get-tuple-element.111), channel_id=1, source_target_pairs={{0,1},{1,0},{2,3},{3,2},{4,5},{5,4},{6,7},{7,6},{8,9},{9,8},{10,11... | collective-permute-start | bytes 1081352 | tf_op jit(solution)/shard_map/ppermute | solution.py:64
  230.3 22.1 %collective-permute-start.46 = (bf16[352,1024]{1,0:T(8,128)(2,1)S(1)}, bf16[352,1024]{1,0:T(8,128)(2,1)S(1)}, u32[]{:S(2)}, u32[]{:S(2)}) collective-permute-start(bf16[352,1024]{1,0:T(8,128)(2,1)S(1)} %add.261), channel_id=1, source_target_pairs={{8,16},{16,8},{9,17},{17,9},{10,18},{18,10},{11,19},{19,11},{12,20... | collective-permute-start | bytes 2162696 | tf_op jit(solution)/shard_map/ppermute | solution.py:92
  232.1 21.9 %collective-permute-start.11 = (bf16[4,256,256]{2,1,0:T(8,128)(2,1)S(1)}, bf16[4,256,256]{2,1,0:T(8,128)(2,1)S(1)}, u32[]{:S(2)}, u32[]{:S(2)}) collective-permute-start(bf16[4,256,256]{2,1,0:T(8,128)(2,1)S(1)} %get-tuple-element.103), channel_id=1, source_target_pairs={{0,1},{1,0},{2,3},{3,2},{4,5},{5,4},{6,7},{7,6},{8,9},{9,8},{10,11... | collective-permute-start | bytes 1572872 | tf_op jit(solution)/shard_map/ppermute | solution.py:64
  237.6 48.8 %collective-permute-start.36 = (bf16[128,2816]{0,1:T(8,128)(2,1)}, bf16[128,2816]{0,1:T(8,128)(2,1)}, u32[]{:S(2)}, u32[]{:S(2)}) collective-permute-start(bf16[128,2816]{0,1:T(8,128)(2,1)} %bitcast.103), channel_id=1, source_target_pairs={{0,8},{24,16},{1,9},{25,17},{2,10},{26,18},{3,11},{27,19},{4,12},{... | collective-permute-start | bytes 2162696 | tf_op jit(solution)/shard_map/ppermute | solution.py:91
  250.3 45.4 %collective-permute-start.42 = (bf16[128,2816]{0,1:T(8,128)(2,1)}, bf16[128,2816]{0,1:T(8,128)(2,1)}, u32[]{:S(2)}, u32[]{:S(2)}) collective-permute-start(bf16[128,2816]{0,1:T(8,128)(2,1)} %bitcast.118), channel_id=1, source_target_pairs={{0,8},{24,16},{1,9},{25,17},{2,10},{26,18},{3,11},{27,19},{4,12},{... | collective-permute-start | bytes 2162696 | tf_op jit(solution)/shard_map/ppermute | solution.py:91
  252.7 53.5 %collective-permute-start.47 = (bf16[352,1024]{1,0:T(8,128)(2,1)S(1)}, bf16[352,1024]{1,0:T(8,128)(2,1)}, u32[]{:S(2)}, u32[]{:S(2)}) collective-permute-start(bf16[352,1024]{1,0:T(8,128)(2,1)S(1)} %add.262), channel_id=1, source_target_pairs={{8,0},{16,24},{9,1},{17,25},{10,2},{18,26},{11,3},{19,27},{12,4},{... | collective-permute-start | bytes 2162696 | tf_op jit(solution)/shard_map/ppermute | solution.py:94
  272.4 25.6 %collective-permute-start.12 = (bf16[4,256,384]{2,1,0:T(8,128)(2,1)S(1)}, bf16[4,256,384]{2,1,0:T(8,128)(2,1)S(1)}, u32[]{:S(2)}, u32[]{:S(2)}) collective-permute-start(bf16[4,256,384]{2,1,0:T(8,128)(2,1)S(1)} %pad_maximum_fusion.13), channel_id=1, source_target_pairs={{0,2},{1,5},{2,0},{3,7},{4,6},{5,1},{6,4},{7,3},{8,10},{9,13},{10,... | collective-permute-start | bytes 2359304 | tf_op jit(solution)/shard_map/ppermute | solution.py:60
  287.9 20.6 %collective-permute-start.37 = (bf16[128,2816]{0,1:T(8,128)(2,1)S(1)}, bf16[128,2816]{0,1:T(8,128)(2,1)S(1)}, u32[]{:S(2)}, u32[]{:S(2)}) collective-permute-start(bf16[128,2816]{0,1:T(8,128)(2,1)S(1)} %bitcast_add_fusion.1), channel_id=1, source_target_pairs={{8,16},{16,8},{9,17},{17,9},{10,18},{18,10},{11,19},{19,11},{12,20... | collective-permute-start | bytes 2162696 | tf_op jit(solution)/shard_map/ppermute | solution.py:92
  308.7 30.5 %collective-permute-start.38 = (bf16[128,2816]{0,1:T(8,128)(2,1)S(1)}, bf16[128,2816]{0,1:T(8,128)(2,1)}, u32[]{:S(2)}, u32[]{:S(2)}) collective-permute-start(bf16[128,2816]{0,1:T(8,128)(2,1)S(1)} %add.257), channel_id=1, source_target_pairs={{8,0},{16,24},{9,1},{17,25},{10,2},{18,26},{11,3},{19,27},{12,4},{... | collective-permute-start | bytes 2162696 | tf_op jit(solution)/shard_map/ppermute | solution.py:94
  310.2 50.8 %collective-permute-start.44 = (bf16[128,2816]{0,1:T(8,128)(2,1)S(1)}, bf16[128,2816]{0,1:T(8,128)(2,1)}, u32[]{:S(2)}, u32[]{:S(2)}) collective-permute-start(bf16[128,2816]{0,1:T(8,128)(2,1)S(1)} %add.259), channel_id=1, source_target_pairs={{8,0},{16,24},{9,1},{17,25},{10,2},{18,26},{11,3},{19,27},{12,4},{... | collective-permute-start | bytes 2162696 | tf_op jit(solution)/shard_map/ppermute | solution.py:94
  313.2 75.1 %collective-permute-start.14 = (bf16[4,256,384]{2,1,0:T(8,128)(2,1)}, bf16[4,256,384]{2,1,0:T(8,128)(2,1)}, u32[]{:S(2)}, u32[]{:S(2)}) collective-permute-start(bf16[4,256,384]{2,1,0:T(8,128)(2,1)} %get-tuple-element.81), channel_id=1, source_target_pairs={{0,1},{1,0},{2,3},{3,2},{4,5},{5,4},{6,7},{7,6},{8,9},{9,8},{10,11... | collective-permute-start | bytes 2359304 | tf_op jit(solution)/shard_map/ppermute | solution.py:64
  315.9 26.3 %collective-permute-start.24 = (bf16[128,1024]{1,0:T(8,128)(2,1)S(1)}, bf16[128,1024]{1,0:T(8,128)(2,1)}, u32[]{:S(2)}, u32[]{:S(2)}) collective-permute-start(bf16[128,1024]{1,0:T(8,128)(2,1)S(1)} %bitcast.270), channel_id=1, source_target_pairs={{0,8},{24,16},{1,9},{25,17},{2,10},{26,18},{3,11},{27,19},{4,12},{... | collective-permute-start | bytes 786440 | tf_op jit(solution)/shard_map/ppermute | solution.py:91
  373.1 29.4 %collective-permute-start.29 = (bf16[128,1024]{1,0:T(8,128)(2,1)S(1)}, bf16[128,1024]{1,0:T(8,128)(2,1)S(1)}, u32[]{:S(2)}, u32[]{:S(2)}) collective-permute-start(bf16[128,1024]{1,0:T(8,128)(2,1)S(1)} %add.252), channel_id=1, source_target_pairs={{8,0},{16,24},{9,1},{17,25},{10,2},{18,26},{11,3},{19,27},{12,4},{... | collective-permute-start | bytes 786440 | tf_op jit(solution)/shard_map/ppermute | solution.py:94
  (59 other events, 604.1 us)
